TPU v7x, 32 devices: a whole 2x2x4 slice. The times are simulated.
32 devices in a mesh: chan: 8 (over y, x, core), slab: 4 (over z).
Axes of the slice: x: 2, y: 2, z: 4, core: 2. Of those that a mesh axis runs over, the one named last changes fastest.
Arguments:
- activations: bfloat16 [128, 8, 8, 128], P('chan', 'slab'), may hold values from -6 to 6
- cotangent: bfloat16 [128, 8, 8, 128], P('chan', 'slab'), may hold values from -6 to 6
- relu_mask: int32 [128, 8, 8, 128], P('chan', 'slab'), may hold values 0 or 1
- weights: bfloat16 [3, 3, 3, 128, 128], replicated, may hold values from -0.109375 to 0.109375
Outputs:
- pre: bfloat16 [128, 8, 8, 128], P('chan', 'slab')
- grad_input: bfloat16 [128, 8, 8, 128], P('chan', 'slab')
All inputs are finite; a program needn't handle non-finite values. No bound on the sum of `relu_mask` on one device may be relied on, other than what follows from the above.
Results may differ from a plain program's by a relative error of at most 0.0013.
Values may be sent and summed in bfloat16 or wider, within the bound.
No kernel may reach another device: no remote copies, remote signals or barrier semaphores. Data moves between devices by JAX's collectives and lax.ppermute only.
A program may use at most 64 MiB of HBM per device.

v0:
```python
import functools
import math

import jax
import jax.numpy as jnp
from jax import lax
from jax.experimental import pallas as pl
from jax.experimental.pallas import tpu as pltpu
from jax.sharding import PartitionSpec as P


LANES = 128
TILE = 16
INPUT_MAX, WEIGHT_MAX = 6.0, 0.109375
CONV_VMEM, ADD_VMEM = 8 << 20, 4 << 20
F32 = jnp.float32
PIECES = 2
ROUNDS = 3


def with_halo(shard, sides, width):
    for axis, dim in sides:
        devices, length = (lax.axis_size(axis), shard.shape[dim])
        up = [(i, (i + 1) % devices) for i in range(devices - 1)]
        down = [(j, i) for i, j in up]
        last = lax.slice_in_dim(shard, length - width, length, axis=dim)
        first = lax.slice_in_dim(shard, 0, width, axis=dim)
        before = lax.ppermute(last, axis, up)
        after = lax.ppermute(first, axis, down)
        shard = jnp.concatenate([before, shard, after], axis=dim)
    return shard


def tap_sum(weights, padded, planes, height, breadth, equation, flipped):
    total = None
    for i in range(3):
        for j in range(3):
            for k in range(3):
                a, b, c = (2 - i, 2 - j, 2 - k) if flipped else (i, j, k)
                window = padded[:, a : a + planes, b : b + height, c : c + breadth]
                term = jnp.einsum(equation, weights[i, j, k], window, preferred_element_type=F32)
                total = term if total is None else total + term
    return total.astype(jnp.bfloat16)


def general_body(activations, cotangent, relu_mask, weights):
    planes, breadth = activations.shape[1], activations.shape[3]
    masked = jnp.where(relu_mask == 1, cotangent, jnp.zeros_like(cotangent))
    stacked = jnp.stack([activations, masked])
    patches = lax.all_to_all(stacked, "chan", split_axis=3, concat_axis=1, tiled=True)
    rimmed = with_halo(patches, (("chan", 3), ("slab", 2)), 1)
    padded = jnp.pad(rimmed, ((0, 0), (0, 0), (0, 0), (0, 0), (1, 1)))
    height = patches.shape[3]
    pre = tap_sum(weights, padded[0], planes, height, breadth, "oi,idhw->odhw", False)
    grad = tap_sum(weights, padded[1], planes, height, breadth, "oi,odhw->idhw", True)
    return tuple(
        lax.all_to_all(block, "chan", split_axis=0, concat_axis=2, tiled=True) for block in (pre, grad)
    )


def window(blocks, a, places):
    sides = []
    for r, p in places:
        pieces = []
        for row in (r - 1, r, r + 1):
            inside = 0 <= row < blocks[0].shape[1]
            pieces += [b[a, row, p] if inside else jnp.zeros(b.shape[3:], b.dtype) for b in blocks]
        sides.append(jnp.concatenate(pieces, axis=0))
    return jnp.concatenate(sides, axis=1)


def columns(taps):
    left, mid, right = taps
    lane = lax.broadcasted_iota(jnp.int32, mid.shape, 1)
    left = jnp.where(lane == 0, 0.0, pltpu.roll(left, 1, 1))
    right = jnp.where(lane == mid.shape[1] - 1, 0.0, pltpu.roll(right, mid.shape[1] - 1, 1))
    return left + mid + right


def all_planes(lhs, blocks, a, r, wanted):
    _, _, planes, width, cols = blocks[0].shape
    y = jnp.dot(lhs, window(blocks, a, [(r, p) for p in range(planes)]), preferred_element_type=F32)

    def part(t, k, p):
        top = (t * 3 + k) * width
        return y[top : top + width, p * cols : (p + 1) * cols]

    def plane(q):
        inputs = [p for p in range(planes) if 0 <= p - q + 1 <= 2]
        return columns([functools.reduce(jnp.add, [part(p - q + 1, k, p) for p in inputs]) for k in range(3)])

    return [plane(q) for q in wanted]


def pack_kernel(act_hbm, cot_hbm, mask_hbm, own_ref, act_ref, cot_ref, mask_ref, turned_ref, sems):
    width, planes, rows, cols = act_ref.shape
    pairs = ((act_hbm, act_ref), (cot_hbm, cot_ref), (mask_hbm, mask_ref))
    step = width // PIECES
    copies = [
        [
            pltpu.make_async_copy(source.at[pl.ds(k * step, step)], target.at[pl.ds(k * step, step)], sems.at[i, k])
            for k in range(PIECES)
        ]
        for i, (source, target) in enumerate(pairs)
    ]
    for i in (2, 0, 1):
        for k in range(PIECES):
            copies[i][k].start()

    def turn(a):
        for p in range(planes):
            value = (act_ref, cot_ref)[a][:, p].astype(F32)
            if a == 1:
                value = jnp.where(mask_ref[:, p] == 1, value, 0.0)
            turned_ref[a, p] = value.reshape(width * rows, cols)
            for r in range(rows):
                own_ref[a, r, p] = turned_ref[a, p, pl.ds(r, width, stride=rows), :].astype(jnp.bfloat16)

    for copy in copies[0]:
        copy.wait()
    turn(0)
    for copy in copies[1] + copies[2]:
        copy.wait()
    turn(1)


def load_kernel(weights_hbm, own_ref, weights_ref, sem):
    copy = pltpu.make_async_copy(weights_hbm, weights_ref, sem)
    copy.start()
    copy.wait()


def early_kernel(count, lhs_ref, *refs):
    blocks, sum_ref = refs[:count], refs[count]
    arrays, rows, planes, width, _ = blocks[0].shape
    depth = 3 * count * width
    for a in range(arrays):
        lhs = lhs_ref[a, :, :depth]
        for r in range(rows):
            for q, value in enumerate(all_planes(lhs, blocks, a, r, range(-1, planes + 1))):
                sum_ref[a, r, q] = value


def edge_kernel(count, start, first, lhs_ref, sum_ref, *refs):
    blocks, edge_ref = refs[:count], refs[count]
    arrays, rows, planes, width, cols = blocks[0].shape
    depth, height = 3 * count * width, 3 * width
    above = (lax.rem(lax.axis_index("slab"), ROUNDS) == 0) == first
    p, q = jnp.where(above, planes - 1, 0), jnp.where(above, planes + 1, 0)
    top = pl.multiple_of(jnp.where(above, 0, 2 * height), TILE)
    for a in range(arrays):
        lhs = lhs_ref[a, pl.ds(top, height), start : start + depth]
        for r in range(0, rows, 2):
            y = jnp.dot(lhs, window(blocks, a, [(r, p), (r + 1, p)]), preferred_element_type=F32)
            for i in range(2):
                taps = [y[k * width : (k + 1) * width, i * cols : (i + 1) * cols] for k in range(3)]
                edge_ref[a, r + i] = columns(taps) + sum_ref[a, r + i, q]


def inner_kernel(count, start, lhs_ref, sum_ref, *refs):
    blocks, inner_ref = refs[:count], refs[count]
    arrays, rows, planes, width, _ = blocks[0].shape
    depth = 3 * count * width
    for a in range(arrays):
        lhs = lhs_ref[a, :, start : start + depth]
        for r in range(rows):
            for p, value in enumerate(all_planes(lhs, blocks, a, r, range(planes))):
                inner_ref[a, r, p] = value + sum_ref[a, r, p + 1]


def add_kernel(inner_ref, *refs):
    edge_refs, (pre_ref, grad_ref, turned_ref) = refs[:ROUNDS], refs[ROUNDS:]
    _, rows, planes, width, cols = inner_ref.shape
    slab = lax.axis_index("slab")
    below, above = slab > 0, slab < lax.axis_size("slab") - 1

    def received(a, r, pair, exists):
        value = edge_refs[0][a, r]
        for j in range(1, ROUNDS):
            value = jnp.where(lax.rem(pair, ROUNDS) == j, edge_refs[j][a, r], value)
        return jnp.where(exists, value, 0.0)

    for a, out_ref in enumerate((pre_ref, grad_ref)):
        for p in range(planes):
            for r in range(rows):
                value = inner_ref[a, r, p]
                if p == 0:
                    value = value + received(a, r, slab + ROUNDS - 1, below)
                if p == planes - 1:
                    value = value + received(a, r, slab, above)
                turned_ref[pl.ds(r, width, stride=rows), :] = value
            out_ref[:, p] = turned_ref[...].reshape(width, rows, cols).astype(jnp.bfloat16)


def aligned_body(activations, cotangent, relu_mask, weights):
    width, planes, rows, cols = activations.shape
    devices, slabs = lax.axis_size("chan"), lax.axis_size("slab")
    channels = width * devices
    own = pl.pallas_call(
        pack_kernel,
        out_shape=jax.ShapeDtypeStruct((2, rows, planes, width, cols), jnp.bfloat16),
        in_specs=[pl.BlockSpec(memory_space=pltpu.HBM)] * 3,
        out_specs=pl.BlockSpec(memory_space=pltpu.VMEM),
        scratch_shapes=[pltpu.VMEM(v.shape, v.dtype) for v in (activations, cotangent, relu_mask)]
        + [pltpu.VMEM((2, planes, width * rows, cols), F32), pltpu.SemaphoreType.DMA((3, PIECES))],
        compiler_params=pltpu.CompilerParams(vmem_limit_bytes=ADD_VMEM),
        name="pack",
    )(*(pltpu.with_memory_space_constraint(v, pltpu.HBM) for v in (activations, cotangent, relu_mask)))

    def swap(value, bit):
        return lax.ppermute(value, "chan", [(i, i ^ bit) for i in range(devices)])

    far = list(range(2, devices, 2))
    last = far.pop()
    early = [0, last]
    far.reverse()
    near = {bit: own if bit == 0 else swap(own, bit) for bit in early + far}

    weights = pl.pallas_call(
        load_kernel,
        out_shape=jax.ShapeDtypeStruct(weights.shape, weights.dtype),
        in_specs=[pl.BlockSpec(memory_space=pltpu.HBM), pl.BlockSpec(memory_space=pl.ANY)],
        out_specs=pl.BlockSpec(memory_space=pltpu.VMEM),
        scratch_shapes=[pltpu.SemaphoreType.DMA],
        compiler_params=pltpu.CompilerParams(vmem_limit_bytes=ADD_VMEM),
        name="load",
    )(pltpu.with_memory_space_constraint(weights, pltpu.HBM), own)

    me = lax.axis_index("chan")
    forward = lax.dynamic_slice_in_dim(weights, me * width, width, 3)
    backward = lax.dynamic_slice_in_dim(weights, me * width, width, 4)[::-1, ::-1, ::-1].swapaxes(3, 4)
    lhs = jnp.stack([forward, backward]).transpose(0, 1, 3, 4, 2, 5)
    lhs = lhs.reshape(2 * 9 * width, 3 * channels)
    column, start = [], 0
    for bits in (early, far):
        start = len(column)
        column += [
            (k, bit, i) for k in range(3) for near_bit in bits for bit in (near_bit, near_bit + 1) for i in range(width)
        ]
        column += [(3, 0, 0)] * (-len(column) % LANES)
    tap, bit, inside = (jnp.array(v, jnp.int32) for v in zip(*column))
    target = tap * channels + jnp.bitwise_xor(bit, me) * width + inside
    target = jnp.where(tap == 3, -1, target)
    order = (lax.broadcasted_iota(jnp.int32, (3 * channels, len(column)), 0) == target[None]).astype(jnp.bfloat16)
    lhs = jnp.dot(lhs, order, preferred_element_type=F32).astype(jnp.bfloat16).reshape(2, 9 * width, len(column))

    near[last], lhs = lax.optimization_barrier((near[last], lhs))
    blocks = {}
    for bit in early + far:
        blocks[bit] = near[bit]
        blocks[bit + 1] = swap(near[bit], 1)
    first = [blocks[bit + i] for bit in early for i in (0, 1)]
    second = [blocks[bit + i] for bit in far for i in (0, 1)]

    def call(kernel, out_shape, *args):
        return pl.pallas_call(
            kernel,
            out_shape=out_shape,
            in_specs=[pl.BlockSpec(memory_space=pltpu.VMEM)] * len(args),
            out_specs=jax.tree.map(lambda _: pl.BlockSpec(memory_space=pltpu.VMEM), out_shape),
            compiler_params=pltpu.CompilerParams(vmem_limit_bytes=CONV_VMEM),
            cost_estimate=pl.CostEstimate(flops=1 << 28, bytes_accessed=1 << 20, transcendentals=0),
        )(*args)

    def sums(*middle):
        return jax.ShapeDtypeStruct((2, rows, *middle, width, cols), F32)

    total = call(functools.partial(early_kernel, len(first)), sums(planes + 2), lhs, *first)
    largest = 9 * channels * INPUT_MAX * WEIGHT_MAX
    scale = 2.0 ** math.floor(math.log2(float(jnp.finfo(jnp.float16).max) / largest))

    def exchange(value, turn):
        partner = {}
        for i in range(turn, slabs - 1, ROUNDS):
            partner[i], partner[i + 1] = i + 1, i
        pairs = [
            (c * slabs + s, c * slabs + partner[s] if s in partner else (c ^ 1) * slabs + s)
            for c in range(devices)
            for s in range(slabs)
        ]
        value = (value * scale).astype(jnp.float16)
        value = lax.ppermute(value, ("chan", "slab"), pairs)
        return value.astype(F32) * (1 / scale)

    sent, other = (
        call(functools.partial(edge_kernel, len(second), start, i == 0), sums(), lhs, total, *second)
        for i in range(2)
    )
    again, other = lax.optimization_barrier((sent, other))
    between = jnp.where(lax.rem(lax.axis_index("slab"), ROUNDS) == 2, again, other)
    edges = [exchange(value, turn) for turn, value in enumerate((sent, between, other))]
    inner = call(functools.partial(inner_kernel, len(second), start), sums(planes), lhs, total, *second)
    out = jax.ShapeDtypeStruct(activations.shape, jnp.bfloat16)
    return tuple(
        pl.pallas_call(
            add_kernel,
            out_shape=(out, out),
            in_specs=[pl.BlockSpec(memory_space=pltpu.VMEM)] * (ROUNDS + 1),
            out_specs=[pl.BlockSpec(memory_space=pltpu.VMEM)] * 2,
            scratch_shapes=[pltpu.VMEM((width * rows, cols), F32)],
            compiler_params=pltpu.CompilerParams(vmem_limit_bytes=ADD_VMEM),
            name="add",
        )(inner, *edges)
    )


def body(activations, cotangent, relu_mask, weights):
    width, planes, rows, cols = activations.shape
    devices = lax.axis_size("chan")
    aligned = (
        width % TILE == 0
        and cols == LANES
        and devices & (devices - 1) == 0
        and devices > 4
        and planes >= 2
        and rows % 8 == 0
        and lax.axis_size("slab") > 1
    )
    if not aligned:
        return general_body(activations, cotangent, relu_mask, weights)
    return aligned_body(activations, cotangent, relu_mask, weights)


def solution(mesh):
    placed = P("chan", "slab", None, None)
    return jax.shard_map(
        body,
        mesh=mesh,
        in_specs=(placed, placed, placed, P()),
        out_specs=(placed, placed),
        check_vma=False,
    )
```

profile of v0, /device:TPU:0, one launch (start us, length us, event | category | flops | bytes accessed | tf_op | source)
XLA Modules:
  0.0 22.3 jit_solution(17548403167928045302)
XLA Ops:
  0.6 1.0 %pack.1.own_ref.refs_0_ = bf16[2,8,2,16,128]{4,3,2,1,0:T(8,128)(2,1)S(1)} custom-call(bf16[16,2,8,128]{3,2,1,0:T(8,128)(2,1)} %act_hbm.1, bf16[16,2,8,128]{3,2,1,0:T(8,128)(2,1)} %cot_hbm.1, s32[16,2,8,128]{3,2,1,0:T(8,128)} %mask_hbm.1), custom_call_target="tpu_custom_call" | custom-call | tf_op jit(solution)/shard_map/pack/pallas_call | solution.py:199
  1.6 4.0 %collective-permute-start = (bf16[2,8,2,16,128]{4,3,2,1,0:T(8,128)(2,1)S(1)}, bf16[2,8,2,16,128]{4,3,2,1,0:T(8,128)(2,1)S(1)}, u32[]{:S(2)}, u32[]{:S(2)}) collective-permute-start(bf16[2,8,2,16,128]{4,3,2,1,0:T(8,128)(2,1)S(1)} %pack.1.own_ref.refs_0_), channel_id=1, source_target_pairs={{0,24},{4,28},{8,16},{12,20},{16,8},{20,12},{24,0},{28,4},{1,25},{... | collective-permute-start | bytes 393224 | tf_op jit(solution)/shard_map/ppermute | solution.py:211
  5.6 0.0 collective-permute-start.1
  5.6 0.5 %collective-permute-start.3 = (bf16[2,8,2,16,128]{4,3,2,1,0:T(8,128)(2,1)S(1)}, bf16[2,8,2,16,128]{4,3,2,1,0:T(8,128)(2,1)S(1)}, u32[]{:S(2)}, u32[]{:S(2)}) collective-permute-start(bf16[2,8,2,16,128]{4,3,2,1,0:T(8,128)(2,1)S(1)} %pack.1.own_ref.refs_0_), channel_id=1, source_target_pairs={{0,16},{4,20},{8,24},{12,28},{16,0},{20,4},{24,8},{28,12},{1,17},{... | collective-permute-start | bytes 393224 | tf_op jit(solution)/shard_map/ppermute | solution.py:211
  6.1 0.2 collective-permute-start.5
  6.3 1.2 %load.1 = bf16[3,3,3,128,128]{4,3,2,1,0:T(8,128)(2,1)S(1)} custom-call(bf16[3,3,3,128,128]{4,3,2,1,0:T(8,128)(2,1)} %weights_hbm.1, bf16[2,8,2,16,128]{4,3,2,1,0:T(8,128)(2,1)S(1)} %pack.1.own_ref.refs_0_), custom_call_target="tpu_custom_call" | custom-call | tf_op jit(solution)/shard_map/load/pallas_call | solution.py:219
  7.5 0.3 %constant_dynamic-slice_fusion = bf16[3,3,3,128,16]{4,3,2,1,0:T(8,128)(2,1)S(1)} fusion(bf16[3,3,3,128,128]{4,3,2,1,0:T(8,128)(2,1)S(1)} %load.1, s32[]{:T(128)S(6)} %select_n.16), kind=kLoop, calls=%fused_computation.15 | loop fusion | bytes 221188 | tf_op jit(solution)/shard_map/dynamic_slice | solution.py:231
  7.9 0.1 reverse_bitcast_fusion
  8.0 0.3 %copy.12 = bf16[1,3,3,3,16,128]{5,4,3,2,1,0:T(8,128)(2,1)S(1)} copy(bf16[1,3,3,3,16,128]{4,5,3,2,1,0:T(8,128)(2,1)S(1)} %reverse_bitcast_fusion) | data formatting | bytes 221184 | tf_op jit(solution)/shard_map/stack | solution.py:232
  8.3 0.0 copy-start
  8.3 0.0 copy-start.1
  8.3 0.0 copy-start.2
  8.3 0.1 copy.13
  8.5 0.5 %copy-done = s32[512]{0:T(512)S(1)} copy-done((s32[512]{0:T(512)S(1)}, s32[512]{0:T(512)}, u32[]{:S(2)}) %copy-start) | copy-done | bytes 2072
  9.0 0.0 copy-done.1
  9.0 0.0 copy-done.2
  9.0 0.4 %convolution_convert_fusion = bf16[288,512]{1,0:T(8,128)(2,1)S(1)} fusion(s32[512]{0:T(512)S(1)} %add_select_fusion, bf16[36,8,3,128]{3,2,1,0:T(4,128)(2,1)S(1)} %bitcast.18), kind=kOutput, calls=%fused_computation | convolution fusion | flops 113590272 | bytes 518144 | tf_op jit(solution)/shard_map/dot_general | solution.py:245
  9.4 0.1 collective-permute-done.refs_2_
  9.5 0.0 collective-permute-start.2
  9.5 2.4 %collective-permute-done.3.refs_0_ = bf16[2,8,2,16,128]{4,3,2,1,0:T(8,128)(2,1)S(1)} collective-permute-done((bf16[2,8,2,16,128]{4,3,2,1,0:T(8,128)(2,1)S(1)}, bf16[2,8,2,16,128]{4,3,2,1,0:T(8,128)(2,1)S(1)}, u32[]{:S(2)}, u32[]{:S(2)}) %collective-permute-start.3) | collective-permute-done | bytes 131104 | tf_op jit(solution)/shard_map/ppermute | solution.py:211
  11.9 0.0 collective-permute-start.4
  11.9 0.2 collective-permute-done.5.refs_2_
  12.2 0.3 %collective-permute-start.6 = (bf16[2,8,2,16,128]{4,3,2,1,0:T(8,128)(2,1)S(1)}, bf16[2,8,2,16,128]{4,3,2,1,0:T(8,128)(2,1)S(1)}, u32[]{:S(2)}, u32[]{:S(2)}) collective-permute-start(bf16[2,8,2,16,128]{4,3,2,1,0:T(8,128)(2,1)S(1)} %collective-permute-done.5.refs_2_), channel_id=1, source_target_pairs={{0,4},{4,0},{8,12},{12,8},{16,20},{20,16},{24,28},{28,24},{1,5},{5... | collective-permute-start | bytes 393224 | tf_op jit(solution)/shard_map/ppermute | solution.py:211
  12.4 0.0 collective-permute-done.1.refs_1_
  12.4 0.0 collective-permute-done.2.refs_3_
  12.4 0.5 %shard_map.86.sum_ref = f32[2,8,4,16,128]{4,3,2,1,0:T(8,128)S(1)} custom-call(bf16[2,144,512]{2,1,0:T(8,128)(2,1)S(1)} %bitcast.14, bf16[2,8,2,16,128]{4,3,2,1,0:T(8,128)(2,1)S(1)} %pack.1.own_ref.refs_0_, bf16[2,8,2,16,128]{4,3,2,1,0:T(8,128)(2,1)S(1)} %collective-permute-done.1.refs_1_, bf16[2,8,2,16,128]{4,3,2,1,0:T(8,128)(2,1)S(1)} %collective-permute-done.refs_2_, ...), custom_call_target="tpu_custom_call" | custom-call | flops 268435456 | bytes 1048576 | tf_op jit(solution)/shard_map/pallas_call | solution.py:256
  13.0 0.3 %collective-permute-done.4.refs_1_ = bf16[2,8,2,16,128]{4,3,2,1,0:T(8,128)(2,1)S(1)} collective-permute-done((bf16[2,8,2,16,128]{4,3,2,1,0:T(8,128)(2,1)S(1)}, bf16[2,8,2,16,128]{4,3,2,1,0:T(8,128)(2,1)S(1)}, u32[]{:S(2)}, u32[]{:S(2)}) %collective-permute-start.4) | collective-permute-done | bytes 131104 | tf_op jit(solution)/shard_map/ppermute | solution.py:211
  13.3 0.2 %collective-permute-done.6.refs_3_ = bf16[2,8,2,16,128]{4,3,2,1,0:T(8,128)(2,1)S(1)} collective-permute-done((bf16[2,8,2,16,128]{4,3,2,1,0:T(8,128)(2,1)S(1)}, bf16[2,8,2,16,128]{4,3,2,1,0:T(8,128)(2,1)S(1)}, u32[]{:S(2)}, u32[]{:S(2)}) %collective-permute-start.6) | collective-permute-done | bytes 131104 | tf_op jit(solution)/shard_map/ppermute | solution.py:211
  13.5 0.3 %shard_map.89 = f32[2,8,16,128]{3,2,1,0:T(8,128)S(1)} custom-call(bf16[2,144,512]{2,1,0:T(8,128)(2,1)S(1)} %bitcast.15, f32[2,8,4,16,128]{4,3,2,1,0:T(8,128)S(1)} %shard_map.86.sum_ref, bf16[2,8,2,16,128]{4,3,2,1,0:T(8,128)(2,1)S(1)} %collective-permute-done.3.refs_0_, bf16[2,8,2,16,128]{4,3,2,1,0:T(8,128)(2,1)S(1)} %collective-permute-done.4.refs_1_, ...), custom_call_target="tpu_custom_call" | custom-call | flops 268435456 | bytes 1048576 | tf_op jit(solution)/shard_map/pallas_call | solution.py:256
  13.8 0.4 %shard_map.88 = f32[2,8,16,128]{3,2,1,0:T(8,128)S(1)} custom-call(bf16[2,144,512]{2,1,0:T(8,128)(2,1)S(1)} %bitcast.16, f32[2,8,4,16,128]{4,3,2,1,0:T(8,128)S(1)} %shard_map.86.sum_ref, bf16[2,8,2,16,128]{4,3,2,1,0:T(8,128)(2,1)S(1)} %collective-permute-done.3.refs_0_, bf16[2,8,2,16,128]{4,3,2,1,0:T(8,128)(2,1)S(1)} %collective-permute-done.4.refs_1_, ...), custom_call_target="tpu_custom_call" | custom-call | flops 268435456 | bytes 1048576 | tf_op jit(solution)/shard_map/pallas_call | solution.py:256
  14.2 0.3 %collective-permute-start.9 = (f16[2,8,16,128]{3,2,1,0:T(8,128)(2,1)S(1)}, f16[2,8,16,128]{3,2,1,0:T(8,128)(2,1)S(1)}, u32[]{:S(2)}, u32[]{:S(2)}) collective-permute-start(f16[2,8,16,128]{3,2,1,0:T(8,128)(2,1)S(1)} %get-tuple-element.10), channel_id=1, source_target_pairs={{0,4},{1,5},{2,3},{3,2},{4,0},{5,1},{6,7},{7,6},{8,12},{9,13},{10,... | collective-permute-start | bytes 196616 | tf_op jit(solution)/shard_map/ppermute | solution.py:282
  14.6 0.3 %collective-permute-start.8 = (f16[2,8,16,128]{3,2,1,0:T(8,128)(2,1)S(1)}, f16[2,8,16,128]{3,2,1,0:T(8,128)(2,1)S(1)}, u32[]{:S(2)}, u32[]{:S(2)}) collective-permute-start(f16[2,8,16,128]{3,2,1,0:T(8,128)(2,1)S(1)} %get-tuple-element.11), channel_id=1, source_target_pairs={{0,4},{1,2},{2,1},{3,7},{4,0},{5,6},{6,5},{7,3},{8,12},{9,10},{10,... | collective-permute-start | bytes 196616 | tf_op jit(solution)/shard_map/ppermute | solution.py:282
  14.9 4.3 %collective-permute-start.7 = (f16[2,8,16,128]{3,2,1,0:T(8,128)(2,1)S(1)}, f16[2,8,16,128]{3,2,1,0:T(8,128)(2,1)S(1)}, u32[]{:S(2)}, u32[]{:S(2)}) collective-permute-start(f16[2,8,16,128]{3,2,1,0:T(8,128)(2,1)S(1)} %multiply_convert_fusion.2), channel_id=1, source_target_pairs={{0,1},{1,0},{2,6},{3,7},{4,5},{5,4},{6,2},{7,3},{8,9},{9,8},{10,14... | collective-permute-start | bytes 196616 | tf_op jit(solution)/shard_map/ppermute | solution.py:282
  19.3 0.5 %shard_map.87.inner_ref = f32[2,8,2,16,128]{4,3,2,1,0:T(8,128)S(1)} custom-call(bf16[2,144,512]{2,1,0:T(8,128)(2,1)S(1)} %bitcast.17, f32[2,8,4,16,128]{4,3,2,1,0:T(8,128)S(1)} %shard_map.86.sum_ref, bf16[2,8,2,16,128]{4,3,2,1,0:T(8,128)(2,1)S(1)} %collective-permute-done.3.refs_0_, bf16[2,8,2,16,128]{4,3,2,1,0:T(8,128)(2,1)S(1)} %collective-permute-done.4.refs_1_, ...), custom_call_target="tpu_custom_call" | custom-call | flops 268435456 | bytes 1048576 | tf_op jit(solution)/shard_map/pallas_call | solution.py:256
  19.8 0.0 collective-permute-done.9
  19.8 0.0 collective-permute-done.8
  19.9 1.6 %collective-permute-done.7 = f16[2,8,16,128]{3,2,1,0:T(8,128)(2,1)S(1)} collective-permute-done((f16[2,8,16,128]{3,2,1,0:T(8,128)(2,1)S(1)}, f16[2,8,16,128]{3,2,1,0:T(8,128)(2,1)S(1)}, u32[]{:S(2)}, u32[]{:S(2)}) %collective-permute-start.7) | collective-permute-done | bytes 65568 | tf_op jit(solution)/shard_map/ppermute | solution.py:282
  21.5 0.7 %add.18 = (bf16[16,2,8,128]{3,2,1,0:T(8,128)(2,1)}, bf16[16,2,8,128]{3,2,1,0:T(8,128)(2,1)}) custom-call(f32[2,8,2,16,128]{4,3,2,1,0:T(8,128)S(1)} %shard_map.87.inner_ref, f32[2,8,16,128]{3,2,1,0:T(8,128)S(1)} %convert_multiply_fusion.2.refs_0_, f32[2,8,16,128]{3,2,1,0:T(8,128)S(1)} %convert_multiply_fusion.1.refs_1_, ...), custom_call_target="tpu_custom_call" | custom-call | tf_op jit(solution)/shard_map/add/pallas_call | solution.py:295
  (8 shorter events, 0.2 us)
Async XLA Ops:
  1.6 7.9 %collective-permute-start = (bf16[2,8,2,16,128]{4,3,2,1,0:T(8,128)(2,1)S(1)}, bf16[2,8,2,16,128]{4,3,2,1,0:T(8,128)(2,1)S(1)}, u32[]{:S(2)}, u32[]{:S(2)}) collective-permute-start(bf16[2,8,2,16,128]{4,3,2,1,0:T(8,128)(2,1)S(1)} %pack.1.own_ref.refs_0_), channel_id=1, source_target_pairs={{0,24},{4,28},{8,16},{12,20},{16,8},{20,12},{24,0},{28,4},{1,25},{... | collective-permute-start | bytes 393224 | tf_op jit(solution)/shard_map/ppermute | solution.py:211
  5.6 6.8 %collective-permute-start.1 = (bf16[2,8,2,16,128]{4,3,2,1,0:T(8,128)(2,1)S(1)}, bf16[2,8,2,16,128]{4,3,2,1,0:T(8,128)(2,1)S(1)}, u32[]{:S(2)}, u32[]{:S(2)}) collective-permute-start(bf16[2,8,2,16,128]{4,3,2,1,0:T(8,128)(2,1)S(1)} %pack.1.own_ref.refs_0_), channel_id=1, source_target_pairs={{0,4},{4,0},{8,12},{12,8},{16,20},{20,16},{24,28},{28,24},{1,5},{5... | collective-permute-start | bytes 393224 | tf_op jit(solution)/shard_map/ppermute | solution.py:211
  5.6 6.3 %collective-permute-start.3 = (bf16[2,8,2,16,128]{4,3,2,1,0:T(8,128)(2,1)S(1)}, bf16[2,8,2,16,128]{4,3,2,1,0:T(8,128)(2,1)S(1)}, u32[]{:S(2)}, u32[]{:S(2)}) collective-permute-start(bf16[2,8,2,16,128]{4,3,2,1,0:T(8,128)(2,1)S(1)} %pack.1.own_ref.refs_0_), channel_id=1, source_target_pairs={{0,16},{4,20},{8,24},{12,28},{16,0},{20,4},{24,8},{28,12},{1,17},{... | collective-permute-start | bytes 393224 | tf_op jit(solution)/shard_map/ppermute | solution.py:211
  6.1 6.0 %collective-permute-start.5 = (bf16[2,8,2,16,128]{4,3,2,1,0:T(8,128)(2,1)S(1)}, bf16[2,8,2,16,128]{4,3,2,1,0:T(8,128)(2,1)S(1)}, u32[]{:S(2)}, u32[]{:S(2)}) collective-permute-start(bf16[2,8,2,16,128]{4,3,2,1,0:T(8,128)(2,1)S(1)} %pack.1.own_ref.refs_0_), channel_id=1, source_target_pairs={{0,8},{4,12},{8,0},{12,4},{16,24},{20,28},{24,16},{28,20},{1,9},{5... | collective-permute-start | bytes 393224 | tf_op jit(solution)/shard_map/ppermute | solution.py:211
  8.3 0.7 %copy-start = (s32[512]{0:T(512)S(1)}, s32[512]{0:T(512)}, u32[]{:S(2)}) copy-start(s32[512]{0:T(512)} %constant.35.clone) | copy-start | bytes 6148
  8.3 0.7 %copy-start.1 = (s32[512]{0:T(512)S(1)}, s32[512]{0:T(512)}, u32[]{:S(2)}) copy-start(s32[512]{0:T(512)} %constant.42) | copy-start | bytes 6148
  8.3 0.7 %copy-start.2 = (pred[512]{0:T(512)(128)(4,1)S(1)}, pred[512]{0:T(512)(128)(4,1)}, u32[]{:S(2)}) copy-start(pred[512]{0:T(512)(128)(4,1)} %constant.40) | copy-start | bytes 1540
  9.5 2.9 %collective-permute-start.2 = (bf16[2,8,2,16,128]{4,3,2,1,0:T(8,128)(2,1)S(1)}, bf16[2,8,2,16,128]{4,3,2,1,0:T(8,128)(2,1)S(1)}, u32[]{:S(2)}, u32[]{:S(2)}) collective-permute-start(bf16[2,8,2,16,128]{4,3,2,1,0:T(8,128)(2,1)S(1)} %collective-permute-done.refs_2_), channel_id=1, source_target_pairs={{0,4},{4,0},{8,12},{12,8},{16,20},{20,16},{24,28},{28,24},{1,5},{5... | collective-permute-start | bytes 393224 | tf_op jit(solution)/shard_map/ppermute | solution.py:211
  11.9 1.3 %collective-permute-start.4 = (bf16[2,8,2,16,128]{4,3,2,1,0:T(8,128)(2,1)S(1)}, bf16[2,8,2,16,128]{4,3,2,1,0:T(8,128)(2,1)S(1)}, u32[]{:S(2)}, u32[]{:S(2)}) collective-permute-start(bf16[2,8,2,16,128]{4,3,2,1,0:T(8,128)(2,1)S(1)} %collective-permute-done.3.refs_0_), channel_id=1, source_target_pairs={{0,4},{4,0},{8,12},{12,8},{16,20},{20,16},{24,28},{28,24},{1,5},{5... | collective-permute-start | bytes 393224 | tf_op jit(solution)/shard_map/ppermute | solution.py:211
  12.2 1.3 %collective-permute-start.6 = (bf16[2,8,2,16,128]{4,3,2,1,0:T(8,128)(2,1)S(1)}, bf16[2,8,2,16,128]{4,3,2,1,0:T(8,128)(2,1)S(1)}, u32[]{:S(2)}, u32[]{:S(2)}) collective-permute-start(bf16[2,8,2,16,128]{4,3,2,1,0:T(8,128)(2,1)S(1)} %collective-permute-done.5.refs_2_), channel_id=1, source_target_pairs={{0,4},{4,0},{8,12},{12,8},{16,20},{20,16},{24,28},{28,24},{1,5},{5... | collective-permute-start | bytes 393224 | tf_op jit(solution)/shard_map/ppermute | solution.py:211
  14.2 5.6 %collective-permute-start.9 = (f16[2,8,16,128]{3,2,1,0:T(8,128)(2,1)S(1)}, f16[2,8,16,128]{3,2,1,0:T(8,128)(2,1)S(1)}, u32[]{:S(2)}, u32[]{:S(2)}) collective-permute-start(f16[2,8,16,128]{3,2,1,0:T(8,128)(2,1)S(1)} %get-tuple-element.10), channel_id=1, source_target_pairs={{0,4},{1,5},{2,3},{3,2},{4,0},{5,1},{6,7},{7,6},{8,12},{9,13},{10,... | collective-permute-start | bytes 196616 | tf_op jit(solution)/shard_map/ppermute | solution.py:282
  14.6 5.2 %collective-permute-start.8 = (f16[2,8,16,128]{3,2,1,0:T(8,128)(2,1)S(1)}, f16[2,8,16,128]{3,2,1,0:T(8,128)(2,1)S(1)}, u32[]{:S(2)}, u32[]{:S(2)}) collective-permute-start(f16[2,8,16,128]{3,2,1,0:T(8,128)(2,1)S(1)} %get-tuple-element.11), channel_id=1, source_target_pairs={{0,4},{1,2},{2,1},{3,7},{4,0},{5,6},{6,5},{7,3},{8,12},{9,10},{10,... | collective-permute-start | bytes 196616 | tf_op jit(solution)/shard_map/ppermute | solution.py:282
  14.9 6.6 %collective-permute-start.7 = (f16[2,8,16,128]{3,2,1,0:T(8,128)(2,1)S(1)}, f16[2,8,16,128]{3,2,1,0:T(8,128)(2,1)S(1)}, u32[]{:S(2)}, u32[]{:S(2)}) collective-permute-start(f16[2,8,16,128]{3,2,1,0:T(8,128)(2,1)S(1)} %multiply_convert_fusion.2), channel_id=1, source_target_pairs={{0,1},{1,0},{2,6},{3,7},{4,5},{5,4},{6,2},{7,3},{8,9},{9,8},{10,14... | collective-permute-start | bytes 196616 | tf_op jit(solution)/shard_map/ppermute | solution.py:282
where the time goes:
time: 22.5 us; the launch traced here: 22.3 us
  starting transfers between devices  10 us (44%)
  waiting for transfers between devices  4.9 us (22%)
  Pallas kernels  4.65 us (21%)
  local copies, waits for them, and re-layouts  1.4 us (6%)
  between operations  0.8 us (4%)
  matrix products  0.37 us (2%)
    ppermute x7, starting transfers between devices, swap(): return lax.ppermute(value, 'chan', [(i, i ^ bit) for i in range(devices)])  5.02 us
    ppermute x3, starting transfers between devices, exchange(): value = lax.ppermute(value, ('chan', 'slab'), pairs)  4.99 us
    ppermute x7, waiting for transfers between devices, swap(): return lax.ppermute(value, 'chan', [(i, i ^ bit) for i in range(devices)])  3.25 us
    pallas_call x4, Pallas kernels, call(): pl.pallas_call(kernel, out_shape=out_shape, in_specs=[pl.BlockSpec(memory...  1.76 us
    ppermute x3, waiting for transfers between devices, exchange(): value = lax.ppermute(value, ('chan', 'slab'), pairs)  1.64 us
    pallas_call x1, Pallas kernels, aligned_body(): pl.pallas_call(load_kernel, out_shape=jax.ShapeDtypeStruct(weights.shape,...  1.17 us
    pallas_call x1, Pallas kernels, aligned_body(): pl.pallas_call(pack_kernel, out_shape=jax.ShapeDtypeStruct((2, rows, plan...  0.97 us
    pallas_call x1, Pallas kernels, aligned_body(): pl.pallas_call(add_kernel, out_shape=(out, out), in_specs=[pl.BlockSpec(m...  0.74 us
  transfers between devices with their start and end apart: 10, of which 6 were waited for; matrix products, arithmetic and copies ran while one was open for 6% of the time, Pallas kernels for 10%

commit v1 on v0

--- a/solution.py
+++ b/solution.py
@@ -141,20 +141,24 @@
                 sum_ref[a, r, q] = value
 
 
-def edge_kernel(count, start, first, lhs_ref, sum_ref, *refs):
-    blocks, edge_ref = refs[:count], refs[count]
+def edge_kernel(count, start, lhs_ref, sum_ref, *refs):
+    blocks, (first_ref, other_ref) = refs[:count], refs[count:]
     arrays, rows, planes, width, cols = blocks[0].shape
-    depth, height = 3 * count * width, 3 * width
-    above = (lax.rem(lax.axis_index("slab"), ROUNDS) == 0) == first
-    p, q = jnp.where(above, planes - 1, 0), jnp.where(above, planes + 1, 0)
-    top = pl.multiple_of(jnp.where(above, 0, 2 * height), TILE)
+    depth = 3 * count * width
+    upward = lax.rem(lax.axis_index("slab"), ROUNDS) == 0
     for a in range(arrays):
-        lhs = lhs_ref[a, pl.ds(top, height), start : start + depth]
-        for r in range(0, rows, 2):
-            y = jnp.dot(lhs, window(blocks, a, [(r, p), (r + 1, p)]), preferred_element_type=F32)
-            for i in range(2):
-                taps = [y[k * width : (k + 1) * width, i * cols : (i + 1) * cols] for k in range(3)]
-                edge_ref[a, r + i] = columns(taps) + sum_ref[a, r + i, q]
+        taps = [lhs_ref[a, t * 3 * width : (t + 1) * 3 * width, start : start + depth] for t in (2, 0)]
+        lhs = jnp.concatenate(taps, axis=0)
+        for r in range(rows):
+            y = jnp.dot(lhs, window(blocks, a, [(r, 0), (r, planes - 1)]), preferred_element_type=F32)
+            below, above = (
+                columns([y[(3 * i + k) * width : (3 * i + k + 1) * width, i * cols : (i + 1) * cols] for k in range(3)])
+                for i in range(2)
+            )
+            below = below + sum_ref[a, r, 0]
+            above = above + sum_ref[a, r, planes + 1]
+            first_ref[a, r] = jnp.where(upward, above, below)
+            other_ref[a, r] = jnp.where(upward, below, above)
 
 
 def inner_kernel(count, start, lhs_ref, sum_ref, *refs):
@@ -282,10 +286,8 @@
         value = lax.ppermute(value, ("chan", "slab"), pairs)
         return value.astype(F32) * (1 / scale)
 
-    sent, other = (
-        call(functools.partial(edge_kernel, len(second), start, i == 0), sums(), lhs, total, *second)
-        for i in range(2)
-    )
+    kernel = functools.partial(edge_kernel, len(second), start)
+    sent, other = call(kernel, (sums(), sums()), lhs, total, *second)
     again, other = lax.optimization_barrier((sent, other))
     between = jnp.where(lax.rem(lax.axis_index("slab"), ROUNDS) == 2, again, other)
     edges = [exchange(value, turn) for turn, value in enumerate((sent, between, other))]

time: 22.5 us -> 22.2 us (0.987)
  Pallas kernels: 4.65 us -> 4.4 us
    pallas_call x4 -> x3, Pallas kernels: 1.76 us -> 1.51 us  [call(): pl.pallas_call(kernel, out_shape=out_shape, in_specs=[pl.BlockSpec(memory...]
where the time goes in v1:
time: 22.2 us; the launch traced here: 22 us
  starting transfers between devices  10 us (45%)
  waiting for transfers between devices  4.9 us (22%)
  Pallas kernels  4.4 us (20%)
  local copies, waits for them, and re-layouts  1.4 us (6%)
  between operations  0.79 us (4%)
  matrix products  0.37 us (2%)
    ppermute x7, starting transfers between devices, swap(): return lax.ppermute(value, 'chan', [(i, i ^ bit) for i in range(devices)])  5.02 us
    ppermute x3, starting transfers between devices, exchange(): value = lax.ppermute(value, ('chan', 'slab'), pairs)  4.99 us
    ppermute x7, waiting for transfers between devices, swap(): return lax.ppermute(value, 'chan', [(i, i ^ bit) for i in range(devices)])  3.25 us
    ppermute x3, waiting for transfers between devices, exchange(): value = lax.ppermute(value, ('chan', 'slab'), pairs)  1.65 us
    pallas_call x3, Pallas kernels, call(): pl.pallas_call(kernel, out_shape=out_shape, in_specs=[pl.BlockSpec(memory...  1.51 us
    pallas_call x1, Pallas kernels, aligned_body(): pl.pallas_call(load_kernel, out_shape=jax.ShapeDtypeStruct(weights.shape,...  1.17 us
    pallas_call x1, Pallas kernels, aligned_body(): pl.pallas_call(pack_kernel, out_shape=jax.ShapeDtypeStruct((2, rows, plan...  0.97 us
    pallas_call x1, Pallas kernels, aligned_body(): pl.pallas_call(add_kernel, out_shape=(out, out), in_specs=[pl.BlockSpec(m...  0.74 us
  transfers between devices with their start and end apart: 10, of which 6 were waited for; matrix products, arithmetic and copies ran while one was open for 6% of the time, Pallas kernels for 10%

profile of v1, /device:TPU:0, one launch (start us, length us, event | category | flops | bytes accessed | tf_op | source)
XLA Modules:
  0.0 22.0 jit_solution(11478702646231125293)
XLA Ops:
  0.6 1.0 %pack.1.own_ref.refs_0_ = bf16[2,8,2,16,128]{4,3,2,1,0:T(8,128)(2,1)S(1)} custom-call(bf16[16,2,8,128]{3,2,1,0:T(8,128)(2,1)} %act_hbm.1, bf16[16,2,8,128]{3,2,1,0:T(8,128)(2,1)} %cot_hbm.1, s32[16,2,8,128]{3,2,1,0:T(8,128)} %mask_hbm.1), custom_call_target="tpu_custom_call" | custom-call | tf_op jit(solution)/shard_map/pack/pallas_call | solution.py:203
  1.6 4.0 %collective-permute-start = (bf16[2,8,2,16,128]{4,3,2,1,0:T(8,128)(2,1)S(1)}, bf16[2,8,2,16,128]{4,3,2,1,0:T(8,128)(2,1)S(1)}, u32[]{:S(2)}, u32[]{:S(2)}) collective-permute-start(bf16[2,8,2,16,128]{4,3,2,1,0:T(8,128)(2,1)S(1)} %pack.1.own_ref.refs_0_), channel_id=1, source_target_pairs={{0,24},{4,28},{8,16},{12,20},{16,8},{20,12},{24,0},{28,4},{1,25},{... | collective-permute-start | bytes 393224 | tf_op jit(solution)/shard_map/ppermute | solution.py:215
  5.6 0.0 collective-permute-start.1
  5.6 0.5 %collective-permute-start.3 = (bf16[2,8,2,16,128]{4,3,2,1,0:T(8,128)(2,1)S(1)}, bf16[2,8,2,16,128]{4,3,2,1,0:T(8,128)(2,1)S(1)}, u32[]{:S(2)}, u32[]{:S(2)}) collective-permute-start(bf16[2,8,2,16,128]{4,3,2,1,0:T(8,128)(2,1)S(1)} %pack.1.own_ref.refs_0_), channel_id=1, source_target_pairs={{0,16},{4,20},{8,24},{12,28},{16,0},{20,4},{24,8},{28,12},{1,17},{... | collective-permute-start | bytes 393224 | tf_op jit(solution)/shard_map/ppermute | solution.py:215
  6.1 0.2 collective-permute-start.5
  6.3 1.2 %load.1 = bf16[3,3,3,128,128]{4,3,2,1,0:T(8,128)(2,1)S(1)} custom-call(bf16[3,3,3,128,128]{4,3,2,1,0:T(8,128)(2,1)} %weights_hbm.1, bf16[2,8,2,16,128]{4,3,2,1,0:T(8,128)(2,1)S(1)} %pack.1.own_ref.refs_0_), custom_call_target="tpu_custom_call" | custom-call | tf_op jit(solution)/shard_map/load/pallas_call | solution.py:223
  7.5 0.3 %constant_dynamic-slice_fusion = bf16[3,3,3,128,16]{4,3,2,1,0:T(8,128)(2,1)S(1)} fusion(bf16[3,3,3,128,128]{4,3,2,1,0:T(8,128)(2,1)S(1)} %load.1, s32[]{:T(128)S(6)} %select_n.16), kind=kLoop, calls=%fused_computation.15 | loop fusion | bytes 221188 | tf_op jit(solution)/shard_map/dynamic_slice | solution.py:235
  7.9 0.1 reverse_bitcast_fusion
  8.0 0.3 %copy.12 = bf16[1,3,3,3,16,128]{5,4,3,2,1,0:T(8,128)(2,1)S(1)} copy(bf16[1,3,3,3,16,128]{4,5,3,2,1,0:T(8,128)(2,1)S(1)} %reverse_bitcast_fusion) | data formatting | bytes 221184 | tf_op jit(solution)/shard_map/stack | solution.py:236
  8.3 0.0 copy-start
  8.3 0.0 copy-start.1
  8.3 0.0 copy-start.2
  8.3 0.1 copy.13
  8.5 0.5 %copy-done = s32[512]{0:T(512)S(1)} copy-done((s32[512]{0:T(512)S(1)}, s32[512]{0:T(512)}, u32[]{:S(2)}) %copy-start) | copy-done | bytes 2072
  9.0 0.0 copy-done.1
  9.0 0.0 copy-done.2
  9.0 0.4 %convolution_convert_fusion = bf16[288,512]{1,0:T(8,128)(2,1)S(1)} fusion(s32[512]{0:T(512)S(1)} %add_select_fusion, bf16[36,8,3,128]{3,2,1,0:T(4,128)(2,1)S(1)} %bitcast.17), kind=kOutput, calls=%fused_computation | convolution fusion | flops 113590272 | bytes 518144 | tf_op jit(solution)/shard_map/dot_general | solution.py:249
  9.4 0.1 collective-permute-done.refs_2_
  9.5 0.0 collective-permute-start.2
  9.5 2.4 %collective-permute-done.3.refs_0_ = bf16[2,8,2,16,128]{4,3,2,1,0:T(8,128)(2,1)S(1)} collective-permute-done((bf16[2,8,2,16,128]{4,3,2,1,0:T(8,128)(2,1)S(1)}, bf16[2,8,2,16,128]{4,3,2,1,0:T(8,128)(2,1)S(1)}, u32[]{:S(2)}, u32[]{:S(2)}) %collective-permute-start.3) | collective-permute-done | bytes 131104 | tf_op jit(solution)/shard_map/ppermute | solution.py:215
  11.9 0.0 collective-permute-start.4
  11.9 0.2 collective-permute-done.5.refs_2_
  12.2 0.3 %collective-permute-start.6 = (bf16[2,8,2,16,128]{4,3,2,1,0:T(8,128)(2,1)S(1)}, bf16[2,8,2,16,128]{4,3,2,1,0:T(8,128)(2,1)S(1)}, u32[]{:S(2)}, u32[]{:S(2)}) collective-permute-start(bf16[2,8,2,16,128]{4,3,2,1,0:T(8,128)(2,1)S(1)} %collective-permute-done.5.refs_2_), channel_id=1, source_target_pairs={{0,4},{4,0},{8,12},{12,8},{16,20},{20,16},{24,28},{28,24},{1,5},{5... | collective-permute-start | bytes 393224 | tf_op jit(solution)/shard_map/ppermute | solution.py:215
  12.4 0.0 collective-permute-done.1.refs_1_
  12.4 0.0 collective-permute-done.2.refs_3_
  12.4 0.5 %shard_map.86.sum_ref = f32[2,8,4,16,128]{4,3,2,1,0:T(8,128)S(1)} custom-call(bf16[2,144,512]{2,1,0:T(8,128)(2,1)S(1)} %bitcast.14, bf16[2,8,2,16,128]{4,3,2,1,0:T(8,128)(2,1)S(1)} %pack.1.own_ref.refs_0_, bf16[2,8,2,16,128]{4,3,2,1,0:T(8,128)(2,1)S(1)} %collective-permute-done.1.refs_1_, bf16[2,8,2,16,128]{4,3,2,1,0:T(8,128)(2,1)S(1)} %collective-permute-done.refs_2_, ...), custom_call_target="tpu_custom_call" | custom-call | flops 268435456 | bytes 1048576 | tf_op jit(solution)/shard_map/pallas_call | solution.py:260
  13.0 0.3 %collective-permute-done.4.refs_1_ = bf16[2,8,2,16,128]{4,3,2,1,0:T(8,128)(2,1)S(1)} collective-permute-done((bf16[2,8,2,16,128]{4,3,2,1,0:T(8,128)(2,1)S(1)}, bf16[2,8,2,16,128]{4,3,2,1,0:T(8,128)(2,1)S(1)}, u32[]{:S(2)}, u32[]{:S(2)}) %collective-permute-start.4) | collective-permute-done | bytes 131104 | tf_op jit(solution)/shard_map/ppermute | solution.py:215
  13.3 0.2 %collective-permute-done.6.refs_3_ = bf16[2,8,2,16,128]{4,3,2,1,0:T(8,128)(2,1)S(1)} collective-permute-done((bf16[2,8,2,16,128]{4,3,2,1,0:T(8,128)(2,1)S(1)}, bf16[2,8,2,16,128]{4,3,2,1,0:T(8,128)(2,1)S(1)}, u32[]{:S(2)}, u32[]{:S(2)}) %collective-permute-start.6) | collective-permute-done | bytes 131104 | tf_op jit(solution)/shard_map/ppermute | solution.py:215
  13.5 0.4 %shard_map.88 = (f32[2,8,16,128]{3,2,1,0:T(8,128)S(1)}, f32[2,8,16,128]{3,2,1,0:T(8,128)S(1)}) custom-call(bf16[2,144,512]{2,1,0:T(8,128)(2,1)S(1)} %bitcast.15, f32[2,8,4,16,128]{4,3,2,1,0:T(8,128)S(1)} %shard_map.86.sum_ref, bf16[2,8,2,16,128]{4,3,2,1,0:T(8,128)(2,1)S(1)} %collective-permute-done.3.refs_0_, ...), custom_call_target="tpu_custom_call" | custom-call | flops 268435456 | bytes 1048576 | tf_op jit(solution)/shard_map/pallas_call | solution.py:260
  14.0 0.3 %collective-permute-start.9 = (f16[2,8,16,128]{3,2,1,0:T(8,128)(2,1)S(1)}, f16[2,8,16,128]{3,2,1,0:T(8,128)(2,1)S(1)}, u32[]{:S(2)}, u32[]{:S(2)}) collective-permute-start(f16[2,8,16,128]{3,2,1,0:T(8,128)(2,1)S(1)} %get-tuple-element.12), channel_id=1, source_target_pairs={{0,4},{1,5},{2,3},{3,2},{4,0},{5,1},{6,7},{7,6},{8,12},{9,13},{10,... | collective-permute-start | bytes 196616 | tf_op jit(solution)/shard_map/ppermute | solution.py:286
  14.3 0.2 %collective-permute-start.8 = (f16[2,8,16,128]{3,2,1,0:T(8,128)(2,1)S(1)}, f16[2,8,16,128]{3,2,1,0:T(8,128)(2,1)S(1)}, u32[]{:S(2)}, u32[]{:S(2)}) collective-permute-start(f16[2,8,16,128]{3,2,1,0:T(8,128)(2,1)S(1)} %get-tuple-element.13), channel_id=1, source_target_pairs={{0,4},{1,2},{2,1},{3,7},{4,0},{5,6},{6,5},{7,3},{8,12},{9,10},{10,... | collective-permute-start | bytes 196616 | tf_op jit(solution)/shard_map/ppermute | solution.py:286
  14.6 4.4 %collective-permute-start.7 = (f16[2,8,16,128]{3,2,1,0:T(8,128)(2,1)S(1)}, f16[2,8,16,128]{3,2,1,0:T(8,128)(2,1)S(1)}, u32[]{:S(2)}, u32[]{:S(2)}) collective-permute-start(f16[2,8,16,128]{3,2,1,0:T(8,128)(2,1)S(1)} %multiply_convert_fusion.2), channel_id=1, source_target_pairs={{0,1},{1,0},{2,6},{3,7},{4,5},{5,4},{6,2},{7,3},{8,9},{9,8},{10,14... | collective-permute-start | bytes 196616 | tf_op jit(solution)/shard_map/ppermute | solution.py:286
  19.0 0.5 %shard_map.87.inner_ref = f32[2,8,2,16,128]{4,3,2,1,0:T(8,128)S(1)} custom-call(bf16[2,144,512]{2,1,0:T(8,128)(2,1)S(1)} %bitcast.16, f32[2,8,4,16,128]{4,3,2,1,0:T(8,128)S(1)} %shard_map.86.sum_ref, bf16[2,8,2,16,128]{4,3,2,1,0:T(8,128)(2,1)S(1)} %collective-permute-done.3.refs_0_, bf16[2,8,2,16,128]{4,3,2,1,0:T(8,128)(2,1)S(1)} %collective-permute-done.4.refs_1_, ...), custom_call_target="tpu_custom_call" | custom-call | flops 268435456 | bytes 1048576 | tf_op jit(solution)/shard_map/pallas_call | solution.py:260
  19.5 0.0 collective-permute-done.9
  19.6 0.0 collective-permute-done.8
  19.6 1.6 %collective-permute-done.7 = f16[2,8,16,128]{3,2,1,0:T(8,128)(2,1)S(1)} collective-permute-done((f16[2,8,16,128]{3,2,1,0:T(8,128)(2,1)S(1)}, f16[2,8,16,128]{3,2,1,0:T(8,128)(2,1)S(1)}, u32[]{:S(2)}, u32[]{:S(2)}) %collective-permute-start.7) | collective-permute-done | bytes 65568 | tf_op jit(solution)/shard_map/ppermute | solution.py:286
  21.3 0.7 %add.18 = (bf16[16,2,8,128]{3,2,1,0:T(8,128)(2,1)}, bf16[16,2,8,128]{3,2,1,0:T(8,128)(2,1)}) custom-call(f32[2,8,2,16,128]{4,3,2,1,0:T(8,128)S(1)} %shard_map.87.inner_ref, f32[2,8,16,128]{3,2,1,0:T(8,128)S(1)} %convert_multiply_fusion.2.refs_0_, f32[2,8,16,128]{3,2,1,0:T(8,128)S(1)} %convert_multiply_fusion.1.refs_1_, ...), custom_call_target="tpu_custom_call" | custom-call | tf_op jit(solution)/shard_map/add/pallas_call | solution.py:297
  (8 shorter events, 0.2 us)
Async XLA Ops:
  1.6 7.9 %collective-permute-start = (bf16[2,8,2,16,128]{4,3,2,1,0:T(8,128)(2,1)S(1)}, bf16[2,8,2,16,128]{4,3,2,1,0:T(8,128)(2,1)S(1)}, u32[]{:S(2)}, u32[]{:S(2)}) collective-permute-start(bf16[2,8,2,16,128]{4,3,2,1,0:T(8,128)(2,1)S(1)} %pack.1.own_ref.refs_0_), channel_id=1, source_target_pairs={{0,24},{4,28},{8,16},{12,20},{16,8},{20,12},{24,0},{28,4},{1,25},{... | collective-permute-start | bytes 393224 | tf_op jit(solution)/shard_map/ppermute | solution.py:215
  5.6 6.8 %collective-permute-start.1 = (bf16[2,8,2,16,128]{4,3,2,1,0:T(8,128)(2,1)S(1)}, bf16[2,8,2,16,128]{4,3,2,1,0:T(8,128)(2,1)S(1)}, u32[]{:S(2)}, u32[]{:S(2)}) collective-permute-start(bf16[2,8,2,16,128]{4,3,2,1,0:T(8,128)(2,1)S(1)} %pack.1.own_ref.refs_0_), channel_id=1, source_target_pairs={{0,4},{4,0},{8,12},{12,8},{16,20},{20,16},{24,28},{28,24},{1,5},{5... | collective-permute-start | bytes 393224 | tf_op jit(solution)/shard_map/ppermute | solution.py:215
  5.6 6.3 %collective-permute-start.3 = (bf16[2,8,2,16,128]{4,3,2,1,0:T(8,128)(2,1)S(1)}, bf16[2,8,2,16,128]{4,3,2,1,0:T(8,128)(2,1)S(1)}, u32[]{:S(2)}, u32[]{:S(2)}) collective-permute-start(bf16[2,8,2,16,128]{4,3,2,1,0:T(8,128)(2,1)S(1)} %pack.1.own_ref.refs_0_), channel_id=1, source_target_pairs={{0,16},{4,20},{8,24},{12,28},{16,0},{20,4},{24,8},{28,12},{1,17},{... | collective-permute-start | bytes 393224 | tf_op jit(solution)/shard_map/ppermute | solution.py:215
  6.1 6.0 %collective-permute-start.5 = (bf16[2,8,2,16,128]{4,3,2,1,0:T(8,128)(2,1)S(1)}, bf16[2,8,2,16,128]{4,3,2,1,0:T(8,128)(2,1)S(1)}, u32[]{:S(2)}, u32[]{:S(2)}) collective-permute-start(bf16[2,8,2,16,128]{4,3,2,1,0:T(8,128)(2,1)S(1)} %pack.1.own_ref.refs_0_), channel_id=1, source_target_pairs={{0,8},{4,12},{8,0},{12,4},{16,24},{20,28},{24,16},{28,20},{1,9},{5... | collective-permute-start | bytes 393224 | tf_op jit(solution)/shard_map/ppermute | solution.py:215
  8.3 0.7 %copy-start = (s32[512]{0:T(512)S(1)}, s32[512]{0:T(512)}, u32[]{:S(2)}) copy-start(s32[512]{0:T(512)} %constant.35.clone) | copy-start | bytes 6148
  8.3 0.7 %copy-start.1 = (s32[512]{0:T(512)S(1)}, s32[512]{0:T(512)}, u32[]{:S(2)}) copy-start(s32[512]{0:T(512)} %constant.42) | copy-start | bytes 6148
  8.3 0.7 %copy-start.2 = (pred[512]{0:T(512)(128)(4,1)S(1)}, pred[512]{0:T(512)(128)(4,1)}, u32[]{:S(2)}) copy-start(pred[512]{0:T(512)(128)(4,1)} %constant.40) | copy-start | bytes 1540
  9.5 2.9 %collective-permute-start.2 = (bf16[2,8,2,16,128]{4,3,2,1,0:T(8,128)(2,1)S(1)}, bf16[2,8,2,16,128]{4,3,2,1,0:T(8,128)(2,1)S(1)}, u32[]{:S(2)}, u32[]{:S(2)}) collective-permute-start(bf16[2,8,2,16,128]{4,3,2,1,0:T(8,128)(2,1)S(1)} %collective-permute-done.refs_2_), channel_id=1, source_target_pairs={{0,4},{4,0},{8,12},{12,8},{16,20},{20,16},{24,28},{28,24},{1,5},{5... | collective-permute-start | bytes 393224 | tf_op jit(solution)/shard_map/ppermute | solution.py:215
  11.9 1.3 %collective-permute-start.4 = (bf16[2,8,2,16,128]{4,3,2,1,0:T(8,128)(2,1)S(1)}, bf16[2,8,2,16,128]{4,3,2,1,0:T(8,128)(2,1)S(1)}, u32[]{:S(2)}, u32[]{:S(2)}) collective-permute-start(bf16[2,8,2,16,128]{4,3,2,1,0:T(8,128)(2,1)S(1)} %collective-permute-done.3.refs_0_), channel_id=1, source_target_pairs={{0,4},{4,0},{8,12},{12,8},{16,20},{20,16},{24,28},{28,24},{1,5},{5... | collective-permute-start | bytes 393224 | tf_op jit(solution)/shard_map/ppermute | solution.py:215
  12.2 1.3 %collective-permute-start.6 = (bf16[2,8,2,16,128]{4,3,2,1,0:T(8,128)(2,1)S(1)}, bf16[2,8,2,16,128]{4,3,2,1,0:T(8,128)(2,1)S(1)}, u32[]{:S(2)}, u32[]{:S(2)}) collective-permute-start(bf16[2,8,2,16,128]{4,3,2,1,0:T(8,128)(2,1)S(1)} %collective-permute-done.5.refs_2_), channel_id=1, source_target_pairs={{0,4},{4,0},{8,12},{12,8},{16,20},{20,16},{24,28},{28,24},{1,5},{5... | collective-permute-start | bytes 393224 | tf_op jit(solution)/shard_map/ppermute | solution.py:215
  14.0 5.6 %collective-permute-start.9 = (f16[2,8,16,128]{3,2,1,0:T(8,128)(2,1)S(1)}, f16[2,8,16,128]{3,2,1,0:T(8,128)(2,1)S(1)}, u32[]{:S(2)}, u32[]{:S(2)}) collective-permute-start(f16[2,8,16,128]{3,2,1,0:T(8,128)(2,1)S(1)} %get-tuple-element.12), channel_id=1, source_target_pairs={{0,4},{1,5},{2,3},{3,2},{4,0},{5,1},{6,7},{7,6},{8,12},{9,13},{10,... | collective-permute-start | bytes 196616 | tf_op jit(solution)/shard_map/ppermute | solution.py:286
  14.3 5.3 %collective-permute-start.8 = (f16[2,8,16,128]{3,2,1,0:T(8,128)(2,1)S(1)}, f16[2,8,16,128]{3,2,1,0:T(8,128)(2,1)S(1)}, u32[]{:S(2)}, u32[]{:S(2)}) collective-permute-start(f16[2,8,16,128]{3,2,1,0:T(8,128)(2,1)S(1)} %get-tuple-element.13), channel_id=1, source_target_pairs={{0,4},{1,2},{2,1},{3,7},{4,0},{5,6},{6,5},{7,3},{8,12},{9,10},{10,... | collective-permute-start | bytes 196616 | tf_op jit(solution)/shard_map/ppermute | solution.py:286
  14.6 6.7 %collective-permute-start.7 = (f16[2,8,16,128]{3,2,1,0:T(8,128)(2,1)S(1)}, f16[2,8,16,128]{3,2,1,0:T(8,128)(2,1)S(1)}, u32[]{:S(2)}, u32[]{:S(2)}) collective-permute-start(f16[2,8,16,128]{3,2,1,0:T(8,128)(2,1)S(1)} %multiply_convert_fusion.2), channel_id=1, source_target_pairs={{0,1},{1,0},{2,6},{3,7},{4,5},{5,4},{6,2},{7,3},{8,9},{9,8},{10,14... | collective-permute-start | bytes 196616 | tf_op jit(solution)/shard_map/ppermute | solution.py:286

commit v2 on v0

--- a/solution.py
+++ b/solution.py
@@ -58,11 +58,11 @@
     )
 
 
-def window(blocks, a, places):
+def window(blocks, a, places, height=3):
     sides = []
     for r, p in places:
         pieces = []
-        for row in (r - 1, r, r + 1):
+        for row in range(r - 1, r - 1 + height):
             inside = 0 <= row < blocks[0].shape[1]
             pieces += [b[a, row, p] if inside else jnp.zeros(b.shape[3:], b.dtype) for b in blocks]
         sides.append(jnp.concatenate(pieces, axis=0))
@@ -141,19 +141,20 @@
                 sum_ref[a, r, q] = value
 
 
-def edge_kernel(count, start, first, lhs_ref, sum_ref, *refs):
+def edge_kernel(count, first, lhs_ref, sum_ref, *refs):
     blocks, edge_ref = refs[:count], refs[count]
     arrays, rows, planes, width, cols = blocks[0].shape
-    depth, height = 3 * count * width, 3 * width
+    height = 3 * width
     above = (lax.rem(lax.axis_index("slab"), ROUNDS) == 0) == first
     p, q = jnp.where(above, planes - 1, 0), jnp.where(above, planes + 1, 0)
     top = pl.multiple_of(jnp.where(above, 0, 2 * height), TILE)
     for a in range(arrays):
-        lhs = lhs_ref[a, pl.ds(top, height), start : start + depth]
-        for r in range(0, rows, 2):
-            y = jnp.dot(lhs, window(blocks, a, [(r, p), (r + 1, p)]), preferred_element_type=F32)
-            for i in range(2):
-                taps = [y[k * width : (k + 1) * width, i * cols : (i + 1) * cols] for k in range(3)]
+        lhs = jnp.concatenate([lhs_ref[a, i, pl.ds(top, height)] for i in range(2)], axis=0)
+        for r in range(0, rows, 4):
+            y = jnp.dot(lhs, window(blocks, a, [(r, p), (r + 2, p)], 4), preferred_element_type=F32)
+            for i in range(4):
+                side, low = y[:, i // 2 * cols : (i // 2 + 1) * cols], i % 2 * height
+                taps = [side[low + k * width : low + (k + 1) * width] for k in range(3)]
                 edge_ref[a, r + i] = columns(taps) + sum_ref[a, r + i, q]
 
 
@@ -243,8 +244,10 @@
     target = jnp.where(tap == 3, -1, target)
     order = (lax.broadcasted_iota(jnp.int32, (3 * channels, len(column)), 0) == target[None]).astype(jnp.bfloat16)
     lhs = jnp.dot(lhs, order, preferred_element_type=F32).astype(jnp.bfloat16).reshape(2, 9 * width, len(column))
-
-    near[last], lhs = lax.optimization_barrier((near[last], lhs))
+    block = 2 * len(far) * width
+    pair = jnp.stack([jnp.pad(lhs[:, :, start : start + 3 * block], ((0, 0), (0, 0), (i * block, block - i * block))) for i in range(2)], axis=1)
+
+    near[last], lhs, pair = lax.optimization_barrier((near[last], lhs, pair))
     blocks = {}
     for bit in early + far:
         blocks[bit] = near[bit]
@@ -283,7 +286,7 @@
         return value.astype(F32) * (1 / scale)
 
     sent, other = (
-        call(functools.partial(edge_kernel, len(second), start, i == 0), sums(), lhs, total, *second)
+        call(functools.partial(edge_kernel, len(second), i == 0), sums(), pair, total, *second)
         for i in range(2)
     )
     again, other = lax.optimization_barrier((sent, other))
@@ -298,7 +301,9 @@
             in_specs=[pl.BlockSpec(memory_space=pltpu.VMEM)] * (ROUNDS + 1),
             out_specs=[pl.BlockSpec(memory_space=pltpu.VMEM)] * 2,
             scratch_shapes=[pltpu.VMEM((width * rows, cols), F32)],
-            compiler_params=pltpu.CompilerParams(vmem_limit_bytes=ADD_VMEM),
+            compiler_params=pltpu.CompilerParams(
+                vmem_limit_bytes=ADD_VMEM, allow_input_fusion=[False] + [True] * ROUNDS
+            ),
             name="add",
         )(inner, *edges)
     )

time: 22.5 us -> 22.4 us (level)
  waiting for transfers between devices: 4.9 us -> 4.61 us
    ppermute x7, waiting for transfers between devices: 3.25 us -> 2.97 us  [swap(): return lax.ppermute(value, 'chan', [(i, i ^ bit) for i in range(devices)])]
  transfers between devices with their start and end apart: 10 -> 10, of which waited for: 6 -> 5; matrix products, arithmetic and copies ran while one was open for 6% -> 7% of each run, Pallas kernels for 10% -> 10%
where the time goes in v2:
time: 22.4 us; the launch traced here: 22.2 us
  starting transfers between devices  10.1 us (45%)
  waiting for transfers between devices  4.61 us (21%)
  Pallas kernels  4.58 us (20%)
  local copies, waits for them, and re-layouts  1.52 us (7%)
  between operations  0.83 us (4%)
  matrix products  0.37 us (2%)
    ppermute x7, starting transfers between devices, swap(): return lax.ppermute(value, 'chan', [(i, i ^ bit) for i in range(devices)])  5.13 us
    ppermute x3, starting transfers between devices, exchange(): value = lax.ppermute(value, ('chan', 'slab'), pairs)  4.99 us
    ppermute x7, waiting for transfers between devices, swap(): return lax.ppermute(value, 'chan', [(i, i ^ bit) for i in range(devices)])  2.97 us
    pallas_call x4, Pallas kernels, call(): pl.pallas_call(kernel, out_shape=out_shape, in_specs=[pl.BlockSpec(memory...  1.7 us
    ppermute x3, waiting for transfers between devices, exchange(): value = lax.ppermute(value, ('chan', 'slab'), pairs)  1.64 us
    pallas_call x1, Pallas kernels, aligned_body(): pl.pallas_call(load_kernel, out_shape=jax.ShapeDtypeStruct(weights.shape,...  1.17 us
    pallas_call x1, Pallas kernels, aligned_body(): pl.pallas_call(pack_kernel, out_shape=jax.ShapeDtypeStruct((2, rows, plan...  0.97 us
    pallas_call x1, Pallas kernels, aligned_body(): pl.pallas_call(add_kernel, out_shape=(out, out), in_specs=[pl.BlockSpec(m...  0.74 us
  transfers between devices with their start and end apart: 10, of which 5 were waited for; matrix products, arithmetic and copies ran while one was open for 7% of the time, Pallas kernels for 10%

profile of v2, /device:TPU:0, one launch (start us, length us, event | category | flops | bytes accessed | tf_op | source)
XLA Modules:
  0.0 22.2 jit_solution(8586100335389584040)
XLA Ops:
  0.6 1.0 %pack.1.own_ref.refs_0_ = bf16[2,8,2,16,128]{4,3,2,1,0:T(8,128)(2,1)S(1)} custom-call(bf16[16,2,8,128]{3,2,1,0:T(8,128)(2,1)} %act_hbm.1, bf16[16,2,8,128]{3,2,1,0:T(8,128)(2,1)} %cot_hbm.1, s32[16,2,8,128]{3,2,1,0:T(8,128)} %mask_hbm.1), custom_call_target="tpu_custom_call" | custom-call | tf_op jit(solution)/shard_map/pack/pallas_call | solution.py:200
  1.6 4.0 %collective-permute-start = (bf16[2,8,2,16,128]{4,3,2,1,0:T(8,128)(2,1)S(1)}, bf16[2,8,2,16,128]{4,3,2,1,0:T(8,128)(2,1)S(1)}, u32[]{:S(2)}, u32[]{:S(2)}) collective-permute-start(bf16[2,8,2,16,128]{4,3,2,1,0:T(8,128)(2,1)S(1)} %pack.1.own_ref.refs_0_), channel_id=1, source_target_pairs={{0,24},{4,28},{8,16},{12,20},{16,8},{20,12},{24,0},{28,4},{1,25},{... | collective-permute-start | bytes 393224 | tf_op jit(solution)/shard_map/ppermute | solution.py:212
  5.6 0.0 collective-permute-start.1
  5.6 0.5 %collective-permute-start.3 = (bf16[2,8,2,16,128]{4,3,2,1,0:T(8,128)(2,1)S(1)}, bf16[2,8,2,16,128]{4,3,2,1,0:T(8,128)(2,1)S(1)}, u32[]{:S(2)}, u32[]{:S(2)}) collective-permute-start(bf16[2,8,2,16,128]{4,3,2,1,0:T(8,128)(2,1)S(1)} %pack.1.own_ref.refs_0_), channel_id=1, source_target_pairs={{0,16},{4,20},{8,24},{12,28},{16,0},{20,4},{24,8},{28,12},{1,17},{... | collective-permute-start | bytes 393224 | tf_op jit(solution)/shard_map/ppermute | solution.py:212
  6.1 0.2 collective-permute-start.5
  6.3 1.2 %load.1 = bf16[3,3,3,128,128]{4,3,2,1,0:T(8,128)(2,1)S(1)} custom-call(bf16[3,3,3,128,128]{4,3,2,1,0:T(8,128)(2,1)} %weights_hbm.1, bf16[2,8,2,16,128]{4,3,2,1,0:T(8,128)(2,1)S(1)} %pack.1.own_ref.refs_0_), custom_call_target="tpu_custom_call" | custom-call | tf_op jit(solution)/shard_map/load/pallas_call | solution.py:220
  7.5 0.3 %constant_dynamic-slice_fusion = bf16[3,3,3,128,16]{4,3,2,1,0:T(8,128)(2,1)S(1)} fusion(bf16[3,3,3,128,128]{4,3,2,1,0:T(8,128)(2,1)S(1)} %load.1, s32[]{:T(128)S(6)} %select_n.16), kind=kLoop, calls=%fused_computation.18 | loop fusion | bytes 221188 | tf_op jit(solution)/shard_map/dynamic_slice | solution.py:232
  7.9 0.1 reverse_bitcast_fusion
  8.0 0.3 %copy.14 = bf16[1,3,3,3,16,128]{5,4,3,2,1,0:T(8,128)(2,1)S(1)} copy(bf16[1,3,3,3,16,128]{4,5,3,2,1,0:T(8,128)(2,1)S(1)} %reverse_bitcast_fusion) | data formatting | bytes 221184 | tf_op jit(solution)/shard_map/stack | solution.py:233
  8.3 0.0 copy-start
  8.3 0.0 copy-start.1
  8.3 0.0 copy-start.2
  8.3 0.1 copy.15
  8.5 0.5 %copy-done = s32[512]{0:T(512)S(1)} copy-done((s32[512]{0:T(512)S(1)}, s32[512]{0:T(512)}, u32[]{:S(2)}) %copy-start) | copy-done | bytes 2072
  9.0 0.0 copy-done.1
  9.0 0.0 copy-done.2
  9.0 0.4 %convolution_convert_fusion = bf16[288,512]{1,0:T(8,128)(2,1)S(1)} fusion(s32[512]{0:T(512)S(1)} %add_select_fusion, bf16[36,8,3,128]{3,2,1,0:T(4,128)(2,1)S(1)} %bitcast.23), kind=kOutput, calls=%fused_computation | convolution fusion | flops 113590272 | bytes 518144 | tf_op jit(solution)/shard_map/dot_general | solution.py:246
  9.4 0.1 pad_bitcast_fusion.1
  9.6 0.0 collective-permute-done.refs_2_
  9.6 0.1 collective-permute-start.2
  9.7 2.2 %collective-permute-done.3.refs_0_ = bf16[2,8,2,16,128]{4,3,2,1,0:T(8,128)(2,1)S(1)} collective-permute-done((bf16[2,8,2,16,128]{4,3,2,1,0:T(8,128)(2,1)S(1)}, bf16[2,8,2,16,128]{4,3,2,1,0:T(8,128)(2,1)S(1)}, u32[]{:S(2)}, u32[]{:S(2)}) %collective-permute-start.3) | collective-permute-done | bytes 131104 | tf_op jit(solution)/shard_map/ppermute | solution.py:212
  11.9 0.0 collective-permute-start.4
  11.9 0.2 collective-permute-done.5.refs_2_
  12.2 0.3 %collective-permute-start.6 = (bf16[2,8,2,16,128]{4,3,2,1,0:T(8,128)(2,1)S(1)}, bf16[2,8,2,16,128]{4,3,2,1,0:T(8,128)(2,1)S(1)}, u32[]{:S(2)}, u32[]{:S(2)}) collective-permute-start(bf16[2,8,2,16,128]{4,3,2,1,0:T(8,128)(2,1)S(1)} %collective-permute-done.5.refs_2_), channel_id=1, source_target_pairs={{0,4},{4,0},{8,12},{12,8},{16,20},{20,16},{24,28},{28,24},{1,5},{5... | collective-permute-start | bytes 393224 | tf_op jit(solution)/shard_map/ppermute | solution.py:212
  12.4 0.0 collective-permute-done.1.refs_1_
  12.4 0.0 collective-permute-done.2.refs_3_
  12.4 0.5 %shard_map.86.sum_ref = f32[2,8,4,16,128]{4,3,2,1,0:T(8,128)S(1)} custom-call(bf16[2,144,512]{2,1,0:T(8,128)(2,1)S(1)} %bitcast.21, bf16[2,8,2,16,128]{4,3,2,1,0:T(8,128)(2,1)S(1)} %pack.1.own_ref.refs_0_, bf16[2,8,2,16,128]{4,3,2,1,0:T(8,128)(2,1)S(1)} %collective-permute-done.1.refs_1_, bf16[2,8,2,16,128]{4,3,2,1,0:T(8,128)(2,1)S(1)} %collective-permute-done.refs_2_, ...), custom_call_target="tpu_custom_call" | custom-call | flops 268435456 | bytes 1048576 | tf_op jit(solution)/shard_map/pallas_call | solution.py:259
  13.0 0.3 %collective-permute-done.4.refs_1_ = bf16[2,8,2,16,128]{4,3,2,1,0:T(8,128)(2,1)S(1)} collective-permute-done((bf16[2,8,2,16,128]{4,3,2,1,0:T(8,128)(2,1)S(1)}, bf16[2,8,2,16,128]{4,3,2,1,0:T(8,128)(2,1)S(1)}, u32[]{:S(2)}, u32[]{:S(2)}) %collective-permute-start.4) | collective-permute-done | bytes 131104 | tf_op jit(solution)/shard_map/ppermute | solution.py:212
  13.3 0.2 %collective-permute-done.6.refs_3_ = bf16[2,8,2,16,128]{4,3,2,1,0:T(8,128)(2,1)S(1)} collective-permute-done((bf16[2,8,2,16,128]{4,3,2,1,0:T(8,128)(2,1)S(1)}, bf16[2,8,2,16,128]{4,3,2,1,0:T(8,128)(2,1)S(1)}, u32[]{:S(2)}, u32[]{:S(2)}) %collective-permute-start.6) | collective-permute-done | bytes 131104 | tf_op jit(solution)/shard_map/ppermute | solution.py:212
  13.5 0.3 %shard_map.89 = f32[2,8,16,128]{3,2,1,0:T(8,128)S(1)} custom-call(bf16[2,2,144,256]{3,2,1,0:T(8,128)(2,1)S(1)} %pad_maximum_fusion.lhs_ref, f32[2,8,4,16,128]{4,3,2,1,0:T(8,128)S(1)} %shard_map.86.sum_ref, bf16[2,8,2,16,128]{4,3,2,1,0:T(8,128)(2,1)S(1)} %collective-permute-done.3.refs_0_, bf16[2,8,2,16,128]{4,3,2,1,0:T(8,128)(2,1)S(1)} %collective-permute-done.4.refs_1_, ...), custom_call_target="tpu_custom_call" | custom-call | flops 268435456 | bytes 1048576 | tf_op jit(solution)/shard_map/pallas_call | solution.py:259
  13.8 0.3 %shard_map.88 = f32[2,8,16,128]{3,2,1,0:T(8,128)S(1)} custom-call(bf16[2,2,144,256]{3,2,1,0:T(8,128)(2,1)S(1)} %pad_maximum_fusion.lhs_ref, f32[2,8,4,16,128]{4,3,2,1,0:T(8,128)S(1)} %shard_map.86.sum_ref, bf16[2,8,2,16,128]{4,3,2,1,0:T(8,128)(2,1)S(1)} %collective-permute-done.3.refs_0_, bf16[2,8,2,16,128]{4,3,2,1,0:T(8,128)(2,1)S(1)} %collective-permute-done.4.refs_1_, ...), custom_call_target="tpu_custom_call" | custom-call | flops 268435456 | bytes 1048576 | tf_op jit(solution)/shard_map/pallas_call | solution.py:259
  14.2 0.3 %collective-permute-start.9 = (f16[2,8,16,128]{3,2,1,0:T(8,128)(2,1)S(1)}, f16[2,8,16,128]{3,2,1,0:T(8,128)(2,1)S(1)}, u32[]{:S(2)}, u32[]{:S(2)}) collective-permute-start(f16[2,8,16,128]{3,2,1,0:T(8,128)(2,1)S(1)} %get-tuple-element.14), channel_id=1, source_target_pairs={{0,4},{1,5},{2,3},{3,2},{4,0},{5,1},{6,7},{7,6},{8,12},{9,13},{10,... | collective-permute-start | bytes 196616 | tf_op jit(solution)/shard_map/ppermute | solution.py:285
  14.5 0.3 %collective-permute-start.8 = (f16[2,8,16,128]{3,2,1,0:T(8,128)(2,1)S(1)}, f16[2,8,16,128]{3,2,1,0:T(8,128)(2,1)S(1)}, u32[]{:S(2)}, u32[]{:S(2)}) collective-permute-start(f16[2,8,16,128]{3,2,1,0:T(8,128)(2,1)S(1)} %get-tuple-element.15), channel_id=1, source_target_pairs={{0,4},{1,2},{2,1},{3,7},{4,0},{5,6},{6,5},{7,3},{8,12},{9,10},{10,... | collective-permute-start | bytes 196616 | tf_op jit(solution)/shard_map/ppermute | solution.py:285
  14.8 4.3 %collective-permute-start.7 = (f16[2,8,16,128]{3,2,1,0:T(8,128)(2,1)S(1)}, f16[2,8,16,128]{3,2,1,0:T(8,128)(2,1)S(1)}, u32[]{:S(2)}, u32[]{:S(2)}) collective-permute-start(f16[2,8,16,128]{3,2,1,0:T(8,128)(2,1)S(1)} %multiply_convert_fusion.2), channel_id=1, source_target_pairs={{0,1},{1,0},{2,6},{3,7},{4,5},{5,4},{6,2},{7,3},{8,9},{9,8},{10,14... | collective-permute-start | bytes 196616 | tf_op jit(solution)/shard_map/ppermute | solution.py:285
  19.2 0.5 %shard_map.87.inner_ref = f32[2,8,2,16,128]{4,3,2,1,0:T(8,128)S(1)} custom-call(bf16[2,144,512]{2,1,0:T(8,128)(2,1)S(1)} %bitcast.22, f32[2,8,4,16,128]{4,3,2,1,0:T(8,128)S(1)} %shard_map.86.sum_ref, bf16[2,8,2,16,128]{4,3,2,1,0:T(8,128)(2,1)S(1)} %collective-permute-done.3.refs_0_, bf16[2,8,2,16,128]{4,3,2,1,0:T(8,128)(2,1)S(1)} %collective-permute-done.4.refs_1_, ...), custom_call_target="tpu_custom_call" | custom-call | flops 268435456 | bytes 1048576 | tf_op jit(solution)/shard_map/pallas_call | solution.py:259
  19.7 0.0 collective-permute-done.9
  19.8 0.0 collective-permute-done.8
  19.8 1.6 %collective-permute-done.7 = f16[2,8,16,128]{3,2,1,0:T(8,128)(2,1)S(1)} collective-permute-done((f16[2,8,16,128]{3,2,1,0:T(8,128)(2,1)S(1)}, f16[2,8,16,128]{3,2,1,0:T(8,128)(2,1)S(1)}, u32[]{:S(2)}, u32[]{:S(2)}) %collective-permute-start.7) | collective-permute-done | bytes 65568 | tf_op jit(solution)/shard_map/ppermute | solution.py:285
  21.5 0.7 %add.22 = (bf16[16,2,8,128]{3,2,1,0:T(8,128)(2,1)}, bf16[16,2,8,128]{3,2,1,0:T(8,128)(2,1)}) custom-call(f32[2,8,2,16,128]{4,3,2,1,0:T(8,128)S(1)} %shard_map.87.inner_ref, f32[2,8,16,128]{3,2,1,0:T(8,128)S(1)} %convert_multiply_fusion.2.refs_0_, f32[2,8,16,128]{3,2,1,0:T(8,128)S(1)} %convert_multiply_fusion.1.refs_1_, ...), custom_call_target="tpu_custom_call" | custom-call | tf_op jit(solution)/shard_map/add/pallas_call | solution.py:298
  (10 shorter events, 0.2 us)
Async XLA Ops:
  1.6 7.9 %collective-permute-start = (bf16[2,8,2,16,128]{4,3,2,1,0:T(8,128)(2,1)S(1)}, bf16[2,8,2,16,128]{4,3,2,1,0:T(8,128)(2,1)S(1)}, u32[]{:S(2)}, u32[]{:S(2)}) collective-permute-start(bf16[2,8,2,16,128]{4,3,2,1,0:T(8,128)(2,1)S(1)} %pack.1.own_ref.refs_0_), channel_id=1, source_target_pairs={{0,24},{4,28},{8,16},{12,20},{16,8},{20,12},{24,0},{28,4},{1,25},{... | collective-permute-start | bytes 393224 | tf_op jit(solution)/shard_map/ppermute | solution.py:212
  5.6 6.8 %collective-permute-start.1 = (bf16[2,8,2,16,128]{4,3,2,1,0:T(8,128)(2,1)S(1)}, bf16[2,8,2,16,128]{4,3,2,1,0:T(8,128)(2,1)S(1)}, u32[]{:S(2)}, u32[]{:S(2)}) collective-permute-start(bf16[2,8,2,16,128]{4,3,2,1,0:T(8,128)(2,1)S(1)} %pack.1.own_ref.refs_0_), channel_id=1, source_target_pairs={{0,4},{4,0},{8,12},{12,8},{16,20},{20,16},{24,28},{28,24},{1,5},{5... | collective-permute-start | bytes 393224 | tf_op jit(solution)/shard_map/ppermute | solution.py:212
  5.6 6.3 %collective-permute-start.3 = (bf16[2,8,2,16,128]{4,3,2,1,0:T(8,128)(2,1)S(1)}, bf16[2,8,2,16,128]{4,3,2,1,0:T(8,128)(2,1)S(1)}, u32[]{:S(2)}, u32[]{:S(2)}) collective-permute-start(bf16[2,8,2,16,128]{4,3,2,1,0:T(8,128)(2,1)S(1)} %pack.1.own_ref.refs_0_), channel_id=1, source_target_pairs={{0,16},{4,20},{8,24},{12,28},{16,0},{20,4},{24,8},{28,12},{1,17},{... | collective-permute-start | bytes 393224 | tf_op jit(solution)/shard_map/ppermute | solution.py:212
  6.1 6.0 %collective-permute-start.5 = (bf16[2,8,2,16,128]{4,3,2,1,0:T(8,128)(2,1)S(1)}, bf16[2,8,2,16,128]{4,3,2,1,0:T(8,128)(2,1)S(1)}, u32[]{:S(2)}, u32[]{:S(2)}) collective-permute-start(bf16[2,8,2,16,128]{4,3,2,1,0:T(8,128)(2,1)S(1)} %pack.1.own_ref.refs_0_), channel_id=1, source_target_pairs={{0,8},{4,12},{8,0},{12,4},{16,24},{20,28},{24,16},{28,20},{1,9},{5... | collective-permute-start | bytes 393224 | tf_op jit(solution)/shard_map/ppermute | solution.py:212
  8.3 0.7 %copy-start = (s32[512]{0:T(512)S(1)}, s32[512]{0:T(512)}, u32[]{:S(2)}) copy-start(s32[512]{0:T(512)} %constant.37.clone) | copy-start | bytes 6148
  8.3 0.7 %copy-start.1 = (s32[512]{0:T(512)S(1)}, s32[512]{0:T(512)}, u32[]{:S(2)}) copy-start(s32[512]{0:T(512)} %constant.48) | copy-start | bytes 6148
  8.3 0.7 %copy-start.2 = (pred[512]{0:T(512)(128)(4,1)S(1)}, pred[512]{0:T(512)(128)(4,1)}, u32[]{:S(2)}) copy-start(pred[512]{0:T(512)(128)(4,1)} %constant.46) | copy-start | bytes 1540
  9.6 2.9 %collective-permute-start.2 = (bf16[2,8,2,16,128]{4,3,2,1,0:T(8,128)(2,1)S(1)}, bf16[2,8,2,16,128]{4,3,2,1,0:T(8,128)(2,1)S(1)}, u32[]{:S(2)}, u32[]{:S(2)}) collective-permute-start(bf16[2,8,2,16,128]{4,3,2,1,0:T(8,128)(2,1)S(1)} %collective-permute-done.refs_2_), channel_id=1, source_target_pairs={{0,4},{4,0},{8,12},{12,8},{16,20},{20,16},{24,28},{28,24},{1,5},{5... | collective-permute-start | bytes 393224 | tf_op jit(solution)/shard_map/ppermute | solution.py:212
  11.9 1.3 %collective-permute-start.4 = (bf16[2,8,2,16,128]{4,3,2,1,0:T(8,128)(2,1)S(1)}, bf16[2,8,2,16,128]{4,3,2,1,0:T(8,128)(2,1)S(1)}, u32[]{:S(2)}, u32[]{:S(2)}) collective-permute-start(bf16[2,8,2,16,128]{4,3,2,1,0:T(8,128)(2,1)S(1)} %collective-permute-done.3.refs_0_), channel_id=1, source_target_pairs={{0,4},{4,0},{8,12},{12,8},{16,20},{20,16},{24,28},{28,24},{1,5},{5... | collective-permute-start | bytes 393224 | tf_op jit(solution)/shard_map/ppermute | solution.py:212
  12.2 1.3 %collective-permute-start.6 = (bf16[2,8,2,16,128]{4,3,2,1,0:T(8,128)(2,1)S(1)}, bf16[2,8,2,16,128]{4,3,2,1,0:T(8,128)(2,1)S(1)}, u32[]{:S(2)}, u32[]{:S(2)}) collective-permute-start(bf16[2,8,2,16,128]{4,3,2,1,0:T(8,128)(2,1)S(1)} %collective-permute-done.5.refs_2_), channel_id=1, source_target_pairs={{0,4},{4,0},{8,12},{12,8},{16,20},{20,16},{24,28},{28,24},{1,5},{5... | collective-permute-start | bytes 393224 | tf_op jit(solution)/shard_map/ppermute | solution.py:212
  14.2 5.6 %collective-permute-start.9 = (f16[2,8,16,128]{3,2,1,0:T(8,128)(2,1)S(1)}, f16[2,8,16,128]{3,2,1,0:T(8,128)(2,1)S(1)}, u32[]{:S(2)}, u32[]{:S(2)}) collective-permute-start(f16[2,8,16,128]{3,2,1,0:T(8,128)(2,1)S(1)} %get-tuple-element.14), channel_id=1, source_target_pairs={{0,4},{1,5},{2,3},{3,2},{4,0},{5,1},{6,7},{7,6},{8,12},{9,13},{10,... | collective-permute-start | bytes 196616 | tf_op jit(solution)/shard_map/ppermute | solution.py:285
  14.5 5.2 %collective-permute-start.8 = (f16[2,8,16,128]{3,2,1,0:T(8,128)(2,1)S(1)}, f16[2,8,16,128]{3,2,1,0:T(8,128)(2,1)S(1)}, u32[]{:S(2)}, u32[]{:S(2)}) collective-permute-start(f16[2,8,16,128]{3,2,1,0:T(8,128)(2,1)S(1)} %get-tuple-element.15), channel_id=1, source_target_pairs={{0,4},{1,2},{2,1},{3,7},{4,0},{5,6},{6,5},{7,3},{8,12},{9,10},{10,... | collective-permute-start | bytes 196616 | tf_op jit(solution)/shard_map/ppermute | solution.py:285
  14.8 6.6 %collective-permute-start.7 = (f16[2,8,16,128]{3,2,1,0:T(8,128)(2,1)S(1)}, f16[2,8,16,128]{3,2,1,0:T(8,128)(2,1)S(1)}, u32[]{:S(2)}, u32[]{:S(2)}) collective-permute-start(f16[2,8,16,128]{3,2,1,0:T(8,128)(2,1)S(1)} %multiply_convert_fusion.2), channel_id=1, source_target_pairs={{0,1},{1,0},{2,6},{3,7},{4,5},{5,4},{6,2},{7,3},{8,9},{9,8},{10,14... | collective-permute-start | bytes 196616 | tf_op jit(solution)/shard_map/ppermute | solution.py:285
